TPU v7x, 32 devices: a whole 2x2x4 slice. The times are simulated.
32 devices in a mesh: areal: 8 (over z, y), layer: 4 (over x, core).
Axes of the slice: x: 2, y: 2, z: 4, core: 2. Of those that a mesh axis runs over, the one named last changes fastest.
Arguments:
- right_side: float32 [3, 16, 64, 256], P(None, 'layer', 'areal'), may hold values from -6 to 6
- diag_blocks: bfloat16 [3, 3, 16, 64, 256], P(None, None, 'layer', 'areal'), may hold values from -3 to 9
- couplings: bfloat16 [6, 3, 3, 16, 64, 256], P(None, None, None, 'layer', 'areal'), may hold values from -1 to 1
- pivot_inverse: bfloat16 [3, 3, 16, 64, 256], P(None, None, 'layer', 'areal'), may hold values from -0.2 to 0.2
- lower_blocks: bfloat16 [3, 3, 16, 64, 256], P(None, None, 'layer', 'areal'), may hold values from -0.1 to 1
- upper_blocks: bfloat16 [3, 3, 16, 64, 256], P(None, None, 'layer', 'areal'), may hold values from -0.1 to 1
- active_cells: int32 [16, 64, 256], P('layer', 'areal'), may hold values 0 or 1
- link_from: int32 [4, 32768], P('layer', 'areal'), may hold values from 0 to 8191
- link_owner: int32 [4, 32768, 1], P('layer', 'areal'), may hold values from 0 to 7; in each aligned block of 4096 rows (0 to 4095, 4096 to 8191, ..., all dimensions but the last counted through in order) at most 1024 rows name the same one
- link_target: int32 [4, 32768], P('layer', 'areal'), may hold values from 0 to 8191
- link_blocks: bfloat16 [3, 3, 4, 32768], P(None, None, 'layer', 'areal'), may hold values from -1.5 to 1.5
Outputs:
- update: float32 [3, 16, 64, 256], P(None, 'layer', 'areal')
- hessenberg: float32 [5, 4], replicated
Inputs may be any that keep to these rules, and one draw needn't show every extreme that they name: `link_owner`: among the 4096 connections listed on one device, at most 1024 name the same owner, and in every draw that number is reached.
All inputs are finite; a program needn't handle non-finite values. No bound on the sum of `active_cells` on one device may be relied on, other than what follows from the above.
Results may differ from a plain program's by a relative error of at most 0.0003.
Values sent between devices are 32-bit elements; how exact they have to be, the bound alone decides.
No kernel may reach another device: no remote copies, remote signals or barrier semaphores. Data moves between devices by JAX's collectives and lax.ppermute only.
A program may use at most 64 MiB of HBM per device.

v0:
```python
import jax
import jax.numpy as jnp
from jax import lax
from jax.sharding import PartitionSpec as P

ITERS = 4
SWEEP_BLOCKS = 2
tiny_square = 1e-06


def passed_along(array, axis, by):
    size = lax.axis_size(axis)
    pairs = [(i, i + by) for i in range(size) if 0 <= i + by < size]
    return lax.ppermute(array, axis, pairs)


def extended(block, sides, width):
    for axis, dim in sides:
        count = lax.axis_size(axis)
        forward = [(i, i + 1) for i in range(count - 1)]
        backward = [(target, source) for source, target in forward]
        low = lax.ppermute(
            lax.slice_in_dim(block, block.shape[dim] - width, None, axis=dim), axis, forward
        )
        high = lax.ppermute(lax.slice_in_dim(block, 0, width, axis=dim), axis, backward)
        block = jnp.concatenate([low, block, high], axis=dim)
    return block


def apply_block(matrix_blocks, vector):
    return jnp.sum(matrix_blocks.astype(jnp.float32) * vector[None], axis=1)


def sweep(values, blocks, downward, incoming):
    layers = values.shape[1]
    ordering = range(layers) if downward else range(layers - 1, -1, -1)
    previous = incoming
    results = [None] * layers
    for layer_at in ordering:
        previous = values[:, layer_at] - apply_block(blocks[:, :, layer_at], previous)
        results[layer_at] = previous
    return jnp.stack(results, axis=1)


def relay_sweep(values, blocks, downward):
    sections = lax.axis_size("layer")
    layer_index = lax.axis_index("layer")
    position = layer_index if downward else sections - 1 - layer_index
    block_rows = values.shape[2] // SWEEP_BLOCKS
    zero_edge = jnp.zeros((3, block_rows, values.shape[3]), jnp.float32)

    def moment(counter, state_pair):
        gathered, incoming = state_pair
        block_at = counter - position
        inside = jnp.logical_and(block_at >= 0, block_at < SWEEP_BLOCKS)
        first_row = jnp.clip(block_at, 0, SWEEP_BLOCKS - 1) * block_rows
        portion = lax.dynamic_slice_in_dim(values, first_row, block_rows, 2)
        coeffs = lax.dynamic_slice_in_dim(blocks, first_row, block_rows, 3)
        solved = sweep(portion, coeffs, downward, incoming)
        gathered = jnp.where(
            inside, lax.dynamic_update_slice_in_dim(gathered, solved, first_row, 2), gathered
        )
        if downward:
            passed = passed_along(solved[:, -1], "layer", 1)
        else:
            passed = passed_along(solved[:, 0], "layer", -1)
        return (gathered, passed)

    final_pair = lax.fori_loop(
        0, sections + SWEEP_BLOCKS - 1, moment, (jnp.zeros_like(values), zero_edge)
    )
    return final_pair[0]


def least_squares(hessenberg, initial):
    columns = hessenberg.shape[1]
    upper_form = hessenberg
    target_vector = jnp.zeros((columns + 1,), jnp.float32).at[0].set(initial)
    cosines = []
    sine_values = []
    for column in range(columns):
        entries = upper_form[:, column]
        for previous in range(column):
            upper_entry = entries[previous]
            lower_entry = entries[previous + 1]
            entries = entries.at[previous].set(
                cosines[previous] * upper_entry + sine_values[previous] * lower_entry
            )
            entries = entries.at[previous + 1].set(
                -sine_values[previous] * upper_entry + cosines[previous] * lower_entry
            )
        upper_entry = entries[column]
        lower_entry = entries[column + 1]
        radius = jnp.sqrt(upper_entry * upper_entry + lower_entry * lower_entry)
        cosines.append(upper_entry / radius)
        sine_values.append(lower_entry / radius)
        entries = entries.at[column].set(radius).at[column + 1].set(0.0)
        upper_form = upper_form.at[:, column].set(entries)
        leading = target_vector[column]
        target_vector = (
            target_vector.at[column]
            .set(cosines[column] * leading)
            .at[column + 1]
            .set(-sine_values[column] * leading)
        )
    solution = [None] * columns
    for row_at in range(columns - 1, -1, -1):
        partial_sum = target_vector[row_at]
        for later_row in range(row_at + 1, columns):
            partial_sum = partial_sum - upper_form[row_at, later_row] * solution[later_row]
        solution[row_at] = partial_sum / upper_form[row_at, row_at]
    return solution


def local(
    right_side,
    diag_blocks,
    couplings,
    pivot_inverse,
    lower_blocks,
    upper_blocks,
    active_cells,
    link_from,
    link_owner,
    link_target,
    link_blocks,
):
    active = active_cells.astype(jnp.float32)
    areal_count = lax.axis_size("areal")
    capacity = 2 * link_from.shape[1] // areal_count
    total_slots = capacity * areal_count
    owners = link_owner[0, :, 0]
    choose = (owners[:, None] == jnp.arange(areal_count, dtype=jnp.int32)[None, :]).astype(
        jnp.int32
    )
    before = jnp.sum((jnp.cumsum(choose, axis=0) - choose) * choose, axis=1)
    slot_of = owners * capacity + before
    outgoing_targets = jnp.zeros((1, total_slots), jnp.int32).at[0, slot_of].set(link_target[0])
    targets = lax.all_to_all(outgoing_targets, "areal", split_axis=1, concat_axis=1, tiled=True)[0]
    sources = link_from[0]
    link_matrix = link_blocks[:, :, 0]
    initial = jnp.sqrt(lax.psum(jnp.sum(right_side * right_side), ("areal", "layer")) + tiny_square)
    basis_list = [right_side / initial]
    directions = []
    hessenberg = jnp.zeros((ITERS + 1, ITERS), jnp.float32)
    for column in range(ITERS):
        scaled = apply_block(pivot_inverse, basis_list[column])
        forward = relay_sweep(scaled, lower_blocks, True)
        direction = relay_sweep(forward, upper_blocks, False)
        directions.append(direction)
        held_cells = direction * active[None]
        padded = extended(held_cells, (("areal", 2), ("layer", 1)), 1)
        padded = jnp.pad(padded, ((0, 0), (0, 0), (0, 0), (1, 1)))
        beside = [
            padded[:, :-2, 1:-1, 1:-1],
            padded[:, 2:, 1:-1, 1:-1],
            padded[:, 1:-1, :-2, 1:-1],
            padded[:, 1:-1, 2:, 1:-1],
            padded[:, 1:-1, 1:-1, :-2],
            padded[:, 1:-1, 1:-1, 2:],
        ]
        flattened = held_cells.reshape(3, -1)
        sending = apply_block(link_matrix, flattened[:, sources])
        outgoing = jnp.zeros((3, total_slots), jnp.float32).at[:, slot_of].set(sending)
        arriving = lax.all_to_all(outgoing, "areal", split_axis=1, concat_axis=1, tiled=True)
        result = apply_block(diag_blocks, held_cells)
        for operate_direction in range(6):
            result = result + apply_block(couplings[operate_direction], beside[operate_direction])
        result = result.reshape(3, -1).at[:, targets].add(arriving).reshape(direction.shape)
        result = active[None] * result + (1.0 - active[None]) * direction
        local_weights = jnp.stack([jnp.sum(earlier * result) for earlier in basis_list])
        weights, own_square = lax.psum(
            (local_weights, jnp.sum(result * result)), ("areal", "layer")
        )
        for position in range(column + 1):
            result = result - weights[position] * basis_list[position]
        length = jnp.sqrt(jnp.maximum(own_square - jnp.sum(weights * weights), 0.0) + tiny_square)
        hessenberg = (
            hessenberg.at[: column + 1, column].set(weights).at[column + 1, column].set(length)
        )
        basis_list.append(result / length)
    coefficients = least_squares(hessenberg, initial)
    update = coefficients[0] * directions[0]
    for position in range(1, ITERS):
        update = update + coefficients[position] * directions[position]
    return (update, hessenberg)


def solution(mesh):
    placed = (
        P(None, "layer", "areal", None),
        P(None, None, "layer", "areal", None),
        P(None, None, None, "layer", "areal", None),
        P(None, None, "layer", "areal", None),
        P(None, None, "layer", "areal", None),
        P(None, None, "layer", "areal", None),
        P("layer", "areal", None),
        P("layer", "areal"),
        P("layer", "areal", None),
        P("layer", "areal"),
        P(None, None, "layer", "areal"),
    )
    return jax.shard_map(
        local,
        mesh=mesh,
        in_specs=placed,
        out_specs=(P(None, "layer", "areal", None), P()),
        check_vma=False,
    )
```

profile of v0, /device:TPU:0, one launch (start us, length us, event | category | flops | bytes accessed | tf_op | source)
XLA Modules:
  0.0 1025.3 jit_solution(16016066879933783754)
XLA Ops:
  2.3 42.2 %psum.63 = f32[]{:T(128)} all-reduce(f32[]{:T(128)} %multiply_reduce_fusion.14), channel_id=1, replica_groups=mesh['areal'=8,'layer'=4] {'areal','layer'}, use_global_device_ids=true, to_apply=%region_1.2 | all-reduce | flops 1 | bytes 8 | tf_op jit(solution)/shard_map/psum | solution.py:142
  47.9 39.3 %while.161 = (s32[]{:T(128)}, f32[3,4,8,256]{3,2,1,0:T(8,128)S(1)}, f32[3,4,256]{2,1,0:T(4,128)S(1)}, s32[]{:T(128)}, f32[3,4,8,256]{3,2,1,0:T(8,128)S(1)}, /*in...) while((s32[]{:T(128)}, f32[3,4,8,256]{3,2,1,0:T(8,128)S(1)}, ...), condition=%wide.region_8.9_spmd, body=%wide.region_3.8_spmd.sunk | while | flops 172047 | bytes 665472 | solution.py:69
  87.3 26.6 %while.162 = (s32[]{:T(128)}, f32[3,4,8,256]{3,2,1,0:T(8,128)S(1)}, f32[3,4,256]{2,1,0:T(4,128)S(1)}, s32[]{:T(128)}, f32[3,4,8,256]{3,2,1,0:T(8,128)S(1)}, /*in...) while((s32[]{:T(128)}, f32[3,4,8,256]{3,2,1,0:T(8,128)S(1)}, ...), condition=%wide.region_14.15_spmd, body=%wide.region_9.14_spmd.sunk | while | flops 172047 | bytes 665472 | solution.py:69
  121.4 16.3 %scatter_custom_fusion.8 = s32[8192]{0:T(1024)} fusion(s32[4096]{0:T(1024)S(1)} %broadcast_select_fusion, s32[4096]{0:T(1024)} %bitcast.782, s32[]{:T(128)} %constant.1186.clone.1), kind=kCustom, calls=%fused_computation.380 | custom fusion | bytes 33280
  146.7 16.3 %gather_fusion = f32[4096,3]{1,0:T(8,128)} fusion(f32[3,8192]{0,1:T(8,128)} %bitcast.749, s32[4096]{0:T(1024)S(1)} %broadcast_clamp_fusion), kind=kCustom, calls=%fused_computation | custom fusion | bytes 114688 | tf_op jit(solution)/shard_map/gather | solution.py:163
  176.1 13.1 %scatter_custom_fusion = f32[3,8192]{0,1:T(8,128)} fusion(s32[4096]{0:T(1024)S(1)} %bitcast.771, f32[4096,3]{1,0:T(8,128)} %copy.146, f32[]{:T(128)} %constant.1184.clone.1), kind=kCustom, calls=%fused_computation.195 | custom fusion | bytes 98816 | tf_op jit(solution)/shard_map/scatter | solution.py:164
  214.0 56.3 %scatter_fusion = f32[3,8192]{0,1:T(8,128)} fusion(f32[3,8192]{0,1:T(8,128)} %bitcast.737, s32[8192]{0:T(1024)S(1)} %bitcast.757, f32[8192,3]{1,0:T(8,128)} %copy.148), kind=kCustom, calls=%fused_computation.5 | custom fusion | flops 24576 | bytes 327680 | tf_op jit(solution)/shard_map/scatter-add | solution.py:169
  273.8 40.0 %all-reduce.9 = (f32[]{:T(128)}, f32[1]{0:T(128)}) all-reduce(f32[]{:T(128)} %get-tuple-element.1555, f32[1]{0:T(128)} %bitcast.155), channel_id=1, replica_groups=mesh['areal'=8,'layer'=4] {'areal','layer'}, use_global_device_ids=true, to_apply=%region_32.33 | all-reduce | flops 2 | bytes 16 | tf_op jit(solution)/shard_map/psum | solution.py:172
  316.6 24.0 %while.163 = (s32[]{:T(128)}, f32[3,4,8,256]{3,2,1,0:T(8,128)S(1)}, f32[3,4,256]{2,1,0:T(4,128)S(1)}, s32[]{:T(128)}, f32[3,4,8,256]{3,2,1,0:T(8,128)S(1)}, /*in...) while((s32[]{:T(128)}, f32[3,4,8,256]{3,2,1,0:T(8,128)S(1)}, ...), condition=%wide.region_40.41_spmd, body=%wide.region_35.40_spmd.sunk | while | flops 172047 | bytes 665472 | solution.py:69
  340.6 26.6 %while.164 = (s32[]{:T(128)}, f32[3,4,8,256]{3,2,1,0:T(8,128)S(1)}, f32[3,4,256]{2,1,0:T(4,128)S(1)}, s32[]{:T(128)}, f32[3,4,8,256]{3,2,1,0:T(8,128)S(1)}, /*in...) while((s32[]{:T(128)}, f32[3,4,8,256]{3,2,1,0:T(8,128)S(1)}, ...), condition=%wide.region_46.47_spmd, body=%wide.region_41.46_spmd.sunk | while | flops 172047 | bytes 665472 | solution.py:69
  374.2 16.3 %gather_fusion.1 = f32[4096,3]{1,0:T(8,128)} fusion(f32[3,8192]{0,1:T(8,128)} %bitcast.752, s32[4096]{0:T(1024)S(1)} %broadcast_clamp_fusion), kind=kCustom, calls=%fused_computation.1 | custom fusion | bytes 114688 | tf_op jit(solution)/shard_map/gather | solution.py:163
  400.2 13.1 %scatter_custom_fusion.2 = f32[3,8192]{0,1:T(8,128)} fusion(s32[4096]{0:T(1024)S(1)} %bitcast.772, f32[4096,3]{1,0:T(8,128)} %copy.155, f32[]{:T(128)} %constant.1184.clone.1), kind=kCustom, calls=%fused_computation.193 | custom fusion | bytes 98816 | tf_op jit(solution)/shard_map/scatter | solution.py:164
  433.6 55.8 %scatter_fusion.1 = f32[3,8192]{0,1:T(8,128)} fusion(f32[3,8192]{0,1:T(8,128)} %bitcast.741, s32[8192]{0:T(1024)S(1)} %bitcast.758, f32[8192,3]{1,0:T(8,128)} %copy.157), kind=kCustom, calls=%fused_computation.7 | custom fusion | flops 24576 | bytes 327680 | tf_op jit(solution)/shard_map/scatter-add | solution.py:169
  494.3 39.7 %all-reduce.8 = (f32[]{:T(128)}, f32[2]{0:T(128)S(1)}) all-reduce(f32[]{:T(128)} %get-tuple-element.1552, f32[2]{0:T(128)S(1)} %pad_maximum_fusion.44), channel_id=1, replica_groups=mesh['areal'=8,'layer'=4] {'areal','layer'}, use_global_device_ids=true, to_apply=%region_61.62 | all-reduce | flops 3 | bytes 24 | tf_op jit(solution)/shard_map/psum | solution.py:172
  538.0 24.0 %while.165 = (s32[]{:T(128)}, f32[3,4,8,256]{3,2,1,0:T(8,128)S(1)}, f32[3,4,256]{2,1,0:T(4,128)S(1)}, s32[]{:T(128)}, f32[3,4,8,256]{3,2,1,0:T(8,128)S(1)}, /*in...) while((s32[]{:T(128)}, f32[3,4,8,256]{3,2,1,0:T(8,128)S(1)}, ...), condition=%wide.region_70.71_spmd, body=%wide.region_65.70_spmd.sunk | while | flops 172047 | bytes 665472 | solution.py:69
  562.1 26.6 %while.166 = (s32[]{:T(128)}, f32[3,4,8,256]{3,2,1,0:T(8,128)S(1)}, f32[3,4,256]{2,1,0:T(4,128)S(1)}, s32[]{:T(128)}, f32[3,4,8,256]{3,2,1,0:T(8,128)S(1)}, /*in...) while((s32[]{:T(128)}, f32[3,4,8,256]{3,2,1,0:T(8,128)S(1)}, ...), condition=%wide.region_76.77_spmd, body=%wide.region_71.0_spmd.sunk | while | flops 172047 | bytes 665472 | solution.py:69
  591.3 16.3 %gather_fusion.2 = f32[4096,3]{1,0:T(8,128)} fusion(f32[3,8192]{0,1:T(8,128)} %bitcast.751, s32[4096]{0:T(1024)S(1)} %broadcast_clamp_fusion), kind=kCustom, calls=%fused_computation.2 | custom fusion | bytes 114688 | tf_op jit(solution)/shard_map/gather | solution.py:163
  653.2 55.8 %scatter_fusion.2 = f32[3,8192]{0,1:T(8,128)} fusion(f32[3,8192]{0,1:T(8,128)} %bitcast.743, s32[8192]{0:T(1024)S(1)} %bitcast.759, f32[8192,3]{1,0:T(8,128)} %copy.166), kind=kCustom, calls=%fused_computation.9 | custom fusion | flops 24576 | bytes 327680 | tf_op jit(solution)/shard_map/scatter-add | solution.py:169
  714.5 44.2 %all-reduce.7 = (f32[]{:T(128)}, f32[3]{0:T(128)S(1)}) all-reduce(f32[]{:T(128)} %get-tuple-element.1548, f32[3]{0:T(128)S(1)} %pad_maximum_fusion.45), channel_id=1, replica_groups=mesh['areal'=8,'layer'=4] {'areal','layer'}, use_global_device_ids=true, to_apply=%region_92.93 | all-reduce | flops 4 | bytes 32 | tf_op jit(solution)/shard_map/psum | solution.py:172
  763.3 24.0 %while.167 = (s32[]{:T(128)}, f32[3,4,8,256]{3,2,1,0:T(8,128)S(1)}, f32[3,4,256]{2,1,0:T(4,128)S(1)}, s32[]{:T(128)}, f32[3,4,8,256]{3,2,1,0:T(8,128)S(1)}, /*in...) while((s32[]{:T(128)}, f32[3,4,8,256]{3,2,1,0:T(8,128)S(1)}, ...), condition=%wide.region_101.102_spmd, body=%wide.region_96.101_spmd.sunk | while | flops 172047 | bytes 665472 | solution.py:69
  787.3 26.6 %while.168 = (s32[]{:T(128)}, f32[3,4,8,256]{3,2,1,0:T(8,128)S(1)}, f32[3,4,256]{2,1,0:T(4,128)S(1)}, s32[]{:T(128)}, f32[3,4,8,256]{3,2,1,0:T(8,128)S(1)}, /*in...) while((s32[]{:T(128)}, f32[3,4,8,256]{3,2,1,0:T(8,128)S(1)}, ...), condition=%wide.region_107.108_spmd, body=%wide.region_102.0_spmd.sunk | while | flops 172047 | bytes 665472 | solution.py:69
  816.6 16.3 %gather_fusion.3 = f32[4096,3]{1,0:T(8,128)} fusion(f32[3,8192]{0,1:T(8,128)} %bitcast.750, s32[4096]{0:T(1024)S(1)} %broadcast_clamp_fusion), kind=kCustom, calls=%fused_computation.3 | custom fusion | bytes 114688 | tf_op jit(solution)/shard_map/gather | solution.py:163
  878.4 55.8 %scatter_fusion.3 = f32[3,8192]{0,1:T(8,128)} fusion(f32[3,8192]{0,1:T(8,128)} %bitcast.739, s32[8192]{0:T(1024)S(1)} %bitcast.760, f32[8192,3]{1,0:T(8,128)} %copy.175), kind=kCustom, calls=%fused_computation.11 | custom fusion | flops 24576 | bytes 327680 | tf_op jit(solution)/shard_map/scatter-add | solution.py:169
  940.4 43.9 %all-reduce.6 = (f32[4]{0:T(128)S(1)}, f32[]{:T(128)}) all-reduce(f32[4]{0:T(128)S(1)} %pad_maximum_fusion.46, f32[]{:T(128)} %get-tuple-element.1542), channel_id=1, replica_groups=mesh['areal'=8,'layer'=4] {'areal','layer'}, use_global_device_ids=true, to_apply=%region_122.123 | all-reduce | flops 5 | bytes 40 | tf_op jit(solution)/shard_map/psum | solution.py:172
  (731 shorter events, 446.6 us)
Async XLA Ops:
  56.6 5.7 collective-permute-start
  92.7 5.6 collective-permute-start.1
  114.0 54.0 %collective-permute-start.8 = (f32[3,4,1,256]{3,2,1,0:T(1,128)S(1)}, f32[3,4,1,256]{3,2,1,0:T(1,128)S(1)}, u32[]{:S(2)}, u32[]{:S(2)}) collective-permute-start(f32[3,4,1,256]{3,2,1,0:T(1,128)S(1)} %get-tuple-element.1733), channel_id=1, source_target_pairs={{0,4},{4,8},{8,12},{12,16},{16,20},{20,24},{24,28},{1,5},{5,9},{9,... | collective-permute-start | bytes 36872 | tf_op jit(solution)/shard_map/ppermute | solution.py:22
  116.7 51.2 %collective-permute-start.9 = (f32[3,4,1,256]{3,2,1,0:T(1,128)S(1)}, f32[3,4,1,256]{3,2,1,0:T(1,128)S(1)}, u32[]{:S(2)}, u32[]{:S(2)}) collective-permute-start(f32[3,4,1,256]{3,2,1,0:T(1,128)S(1)} %get-tuple-element.1734), channel_id=1, source_target_pairs={{4,0},{8,4},{12,8},{16,12},{20,16},{24,20},{28,24},{5,1},{9,5},{13... | collective-permute-start | bytes 36872 | tf_op jit(solution)/shard_map/ppermute | solution.py:25
  137.7 60.2 %all-to-all-start = ((s32[1,8,1024]{2,0,1:T(1,128)}), s32[1,8,1024]{2,0,1:T(1,128)S(1)}, u32[]{:S(2)}, u32[]{:S(2)}) async-start(s32[1,8,1024]{2,0,1:T(1,128)} %bitcast.141), calls=%async_computation | async-start | bytes 65536 | tf_op jit(solution)/shard_map/all_to_all | solution.py:139
  168.0 26.6 %collective-permute-start.10 = (f32[3,1,10,256]{3,2,1,0:T(8,128)S(1)}, f32[3,1,10,256]{3,2,1,0:T(8,128)S(1)}, u32[]{:S(2)}, u32[]{:S(2)}) collective-permute-start(f32[3,1,10,256]{3,2,1,0:T(8,128)S(1)} %get-tuple-element.1718), channel_id=1, source_target_pairs={{0,1},{1,2},{2,3},{4,5},{5,6},{6,7},{8,9},{9,10},{10,11},{12,13},{... | collective-permute-start | bytes 92168 | tf_op jit(solution)/shard_map/ppermute | solution.py:22
  171.5 23.1 %collective-permute-start.11 = (f32[3,1,10,256]{3,2,1,0:T(8,128)S(1)}, f32[3,1,10,256]{3,2,1,0:T(8,128)S(1)}, u32[]{:S(2)}, u32[]{:S(2)}) collective-permute-start(f32[3,1,10,256]{3,2,1,0:T(8,128)S(1)} %get-tuple-element.1717), channel_id=1, source_target_pairs={{1,0},{2,1},{3,2},{5,4},{6,5},{7,6},{9,8},{10,9},{11,10},{13,12},{... | collective-permute-start | bytes 92168 | tf_op jit(solution)/shard_map/ppermute | solution.py:25
  197.8 13.5 %all-to-all-start.1 = ((f32[3,8,1024]{2,0,1:T(4,128)}), f32[3,8,1024]{2,0,1:T(4,128)S(1)}, u32[]{:S(2)}, u32[]{:S(2)}) async-start(f32[3,8,1024]{2,0,1:T(4,128)} %copy.147), calls=%async_computation.1 | async-start | bytes 262144 | tf_op jit(solution)/shard_map/all_to_all | solution.py:165
  319.2 5.7 collective-permute-start.2
  367.2 25.4 %collective-permute-start.12 = (f32[3,4,1,256]{3,2,1,0:T(1,128)S(1)}, f32[3,4,1,256]{3,2,1,0:T(1,128)S(1)}, u32[]{:S(2)}, u32[]{:S(2)}) collective-permute-start(f32[3,4,1,256]{3,2,1,0:T(1,128)S(1)} %get-tuple-element.1731), channel_id=1, source_target_pairs={{0,4},{4,8},{8,12},{12,16},{16,20},{20,24},{24,28},{1,5},{5,9},{9,... | collective-permute-start | bytes 36872 | tf_op jit(solution)/shard_map/ppermute | solution.py:22
  370.3 22.4 %collective-permute-start.13 = (f32[3,4,1,256]{3,2,1,0:T(1,128)S(1)}, f32[3,4,1,256]{3,2,1,0:T(1,128)S(1)}, u32[]{:S(2)}, u32[]{:S(2)}) collective-permute-start(f32[3,4,1,256]{3,2,1,0:T(1,128)S(1)} %get-tuple-element.1732), channel_id=1, source_target_pairs={{4,0},{8,4},{12,8},{16,12},{20,16},{24,20},{28,24},{5,1},{9,5},{13... | collective-permute-start | bytes 36872 | tf_op jit(solution)/shard_map/ppermute | solution.py:25
  392.7 30.8 %collective-permute-start.14 = (f32[3,1,10,256]{3,2,1,0:T(8,128)S(1)}, f32[3,1,10,256]{3,2,1,0:T(8,128)S(1)}, u32[]{:S(2)}, u32[]{:S(2)}) collective-permute-start(f32[3,1,10,256]{3,2,1,0:T(8,128)S(1)} %get-tuple-element.1714), channel_id=1, source_target_pairs={{0,1},{1,2},{2,3},{4,5},{5,6},{6,7},{8,9},{9,10},{10,11},{12,13},{... | collective-permute-start | bytes 92168 | tf_op jit(solution)/shard_map/ppermute | solution.py:22
  396.8 26.8 %collective-permute-start.15 = (f32[3,1,10,256]{3,2,1,0:T(8,128)S(1)}, f32[3,1,10,256]{3,2,1,0:T(8,128)S(1)}, u32[]{:S(2)}, u32[]{:S(2)}) collective-permute-start(f32[3,1,10,256]{3,2,1,0:T(8,128)S(1)} %get-tuple-element.1713), channel_id=1, source_target_pairs={{1,0},{2,1},{3,2},{5,4},{6,5},{7,6},{9,8},{10,9},{11,10},{13,12},{... | collective-permute-start | bytes 92168 | tf_op jit(solution)/shard_map/ppermute | solution.py:25
  416.7 14.3 %all-to-all-start.2 = ((f32[3,8,1024]{2,0,1:T(4,128)}), f32[3,8,1024]{2,0,1:T(4,128)S(1)}, u32[]{:S(2)}, u32[]{:S(2)}) async-start(f32[3,8,1024]{2,0,1:T(4,128)} %copy.156), calls=%async_computation.2 | async-start | bytes 262144 | tf_op jit(solution)/shard_map/all_to_all | solution.py:165
  540.6 5.7 collective-permute-start.4
  609.8 29.0 %collective-permute-start.16 = (f32[3,4,1,256]{3,2,1,0:T(1,128)S(1)}, f32[3,4,1,256]{3,2,1,0:T(1,128)S(1)}, u32[]{:S(2)}, u32[]{:S(2)}) collective-permute-start(f32[3,4,1,256]{3,2,1,0:T(1,128)S(1)} %get-tuple-element.1729), channel_id=1, source_target_pairs={{0,4},{4,8},{8,12},{12,16},{16,20},{20,24},{24,28},{1,5},{5,9},{9,... | collective-permute-start | bytes 36872 | tf_op jit(solution)/shard_map/ppermute | solution.py:22
  612.2 26.7 %collective-permute-start.17 = (f32[3,4,1,256]{3,2,1,0:T(1,128)S(1)}, f32[3,4,1,256]{3,2,1,0:T(1,128)S(1)}, u32[]{:S(2)}, u32[]{:S(2)}) collective-permute-start(f32[3,4,1,256]{3,2,1,0:T(1,128)S(1)} %get-tuple-element.1730), channel_id=1, source_target_pairs={{4,0},{8,4},{12,8},{16,12},{20,16},{24,20},{28,24},{5,1},{9,5},{13... | collective-permute-start | bytes 36872 | tf_op jit(solution)/shard_map/ppermute | solution.py:25
  632.1 18.4 %all-to-all-start.3 = ((f32[3,8,1024]{2,0,1:T(4,128)}), f32[3,8,1024]{2,0,1:T(4,128)S(1)}, u32[]{:S(2)}, u32[]{:S(2)}) async-start(f32[3,8,1024]{2,0,1:T(4,128)} %copy.165), calls=%async_computation.3 | async-start | bytes 262144 | tf_op jit(solution)/shard_map/all_to_all | solution.py:165
  638.9 8.3 collective-permute-start.18
  765.9 5.7 collective-permute-start.6
  835.1 29.0 %collective-permute-start.20 = (f32[3,4,1,256]{3,2,1,0:T(1,128)S(1)}, f32[3,4,1,256]{3,2,1,0:T(1,128)S(1)}, u32[]{:S(2)}, u32[]{:S(2)}) collective-permute-start(f32[3,4,1,256]{3,2,1,0:T(1,128)S(1)} %get-tuple-element.1727), channel_id=1, source_target_pairs={{0,4},{4,8},{8,12},{12,16},{16,20},{20,24},{24,28},{1,5},{5,9},{9,... | collective-permute-start | bytes 36872 | tf_op jit(solution)/shard_map/ppermute | solution.py:22
  837.2 26.8 %collective-permute-start.21 = (f32[3,4,1,256]{3,2,1,0:T(1,128)S(1)}, f32[3,4,1,256]{3,2,1,0:T(1,128)S(1)}, u32[]{:S(2)}, u32[]{:S(2)}) collective-permute-start(f32[3,4,1,256]{3,2,1,0:T(1,128)S(1)} %get-tuple-element.1728), channel_id=1, source_target_pairs={{4,0},{8,4},{12,8},{16,12},{20,16},{24,20},{28,24},{5,1},{9,5},{13... | collective-permute-start | bytes 36872 | tf_op jit(solution)/shard_map/ppermute | solution.py:25
  857.2 18.6 %all-to-all-start.4 = ((f32[3,8,1024]{2,0,1:T(4,128)}), f32[3,8,1024]{2,0,1:T(4,128)S(1)}, u32[]{:S(2)}, u32[]{:S(2)}) async-start(f32[3,8,1024]{2,0,1:T(4,128)} %copy.174), calls=%async_computation.4 | async-start | bytes 262144 | tf_op jit(solution)/shard_map/all_to_all | solution.py:165
  864.1 8.3 collective-permute-start.22
  (52 other events, 1162.2 us)
where the time goes:
time: 1040 us; the launch traced here: 1030 us
  other arithmetic  286 us (28%)
  local copies, waits for them, and re-layouts  223 us (21%)
  blocking collectives  210 us (20%)
  starting transfers between devices  168 us (16%)
  waiting for transfers between devices  101 us (10%)
  between operations  34.5 us (3%)
    scatter-add x4, other arithmetic, local(): result.reshape(3, -1).at[:, targets].add(arriving).reshape(direction.shape)  224 us
    psum x4, blocking collectives, local(): lax.psum((local_weights, jnp.sum(result * result)), ('areal', 'layer'))  168 us
    ppermute x40, starting transfers between devices, passed_along(): return lax.ppermute(array, axis, pairs)  101 us
    ppermute x40, waiting for transfers between devices, passed_along(): return lax.ppermute(array, axis, pairs)  88.8 us
    gather x8, local copies, waits for them, and re-layouts, local(): sending = apply_block(link_matrix, flattened[:, sources])  73.9 us
    scatter x4, local copies, waits for them, and re-layouts, local(): jnp.zeros((3, total_slots), jnp.float32).at[:, slot_of].set(sending)  52.2 us
    psum x1, blocking collectives, local(): lax.psum(jnp.sum(right_side * right_side), ('areal', 'layer')) + tiny_square  42.2 us
    all_to_all x4, starting transfers between devices, local(): lax.all_to_all(outgoing, 'areal', split_axis=1, concat_axis=1, tiled=True)  25.3 us
  transfers between devices with their start and end apart: 61, of which 42 were waited for; matrix products, arithmetic and copies ran while one was open for 16% of the time, Pallas kernels for 0%

commit v1 on v0

--- a/solution.py
+++ b/solution.py
@@ -6,6 +6,11 @@
 ITERS = 4
 SWEEP_BLOCKS = 2
 tiny_square = 1e-06
+
+
+def convert_the_table(local_block, shard_axis, ax_name):
+    view_out = jax.lax.psum(local_block, axis_name=shard_axis)
+    return jax.lax.psum(view_out, axis_name=ax_name)
 
 
 def passed_along(array, axis, by):
@@ -169,8 +174,8 @@
         result = result.reshape(3, -1).at[:, targets].add(arriving).reshape(direction.shape)
         result = active[None] * result + (1.0 - active[None]) * direction
         local_weights = jnp.stack([jnp.sum(earlier * result) for earlier in basis_list])
-        weights, own_square = lax.psum(
-            (local_weights, jnp.sum(result * result)), ("areal", "layer")
+        weights, own_square = convert_the_table(
+            (local_weights, jnp.sum(result * result)), "layer", "areal"
         )
         for position in range(column + 1):
             result = result - weights[position] * basis_list[position]

time: 1040 us -> 977 us (0.939)
  blocking collectives: 210 us -> 159 us
    psum x4 -> x8, blocking collectives: 168 us -> 117 us  [the longest x4 85.5 us: convert_the_table(): return jax.lax.psum(view_out, axis_name=ax_name)]
  transfers between devices with their start and end apart: 61 -> 61, of which waited for: 42 -> 42; matrix products, arithmetic and copies ran while one was open for 16% -> 17% of each run, Pallas kernels for 0% -> 0%
where the time goes in v1:
time: 977 us; the launch traced here: 964 us
  other arithmetic  286 us (29%)
  local copies, waits for them, and re-layouts  223 us (23%)
  blocking collectives  159 us (16%)
  starting transfers between devices  158 us (16%)
  waiting for transfers between devices  101 us (10%)
  between operations  34.4 us (4%)
    scatter-add x4, other arithmetic, local(): result.reshape(3, -1).at[:, targets].add(arriving).reshape(direction.shape)  223 us
    ppermute x40, starting transfers between devices, passed_along(): return lax.ppermute(array, axis, pairs)  101 us
    ppermute x40, waiting for transfers between devices, passed_along(): return lax.ppermute(array, axis, pairs)  88.8 us
    psum x4, blocking collectives, convert_the_table(): return jax.lax.psum(view_out, axis_name=ax_name)  85.5 us
    gather x8, local copies, waits for them, and re-layouts, local(): sending = apply_block(link_matrix, flattened[:, sources])  73.9 us
    scatter x4, local copies, waits for them, and re-layouts, local(): jnp.zeros((3, total_slots), jnp.float32).at[:, slot_of].set(sending)  52.4 us
    psum x1, blocking collectives, local(): lax.psum(jnp.sum(right_side * right_side), ('areal', 'layer')) + tiny_square  42.2 us
    psum x4, blocking collectives, convert_the_table(): view_out = jax.lax.psum(local_block, axis_name=shard_axis)  31.3 us
  transfers between devices with their start and end apart: 61, of which 42 were waited for; matrix products, arithmetic and copies ran while one was open for 17% of the time, Pallas kernels for 0%

profile of v1, /device:TPU:0, one launch (start us, length us, event | category | flops | bytes accessed | tf_op | source)
XLA Modules:
  0.0 963.9 jit_solution(878828919884726091)
XLA Ops:
  2.3 42.2 %psum.119 = f32[]{:T(128)} all-reduce(f32[]{:T(128)} %multiply_reduce_fusion.14), channel_id=1, replica_groups=mesh['areal'=8,'layer'=4] {'areal','layer'}, use_global_device_ids=true, to_apply=%region_1.2 | all-reduce | flops 1 | bytes 8 | tf_op jit(solution)/shard_map/psum | solution.py:147
  47.9 39.3 %while.161 = (s32[]{:T(128)}, f32[3,4,8,256]{3,2,1,0:T(8,128)S(1)}, f32[3,4,256]{2,1,0:T(4,128)S(1)}, s32[]{:T(128)}, f32[3,4,8,256]{3,2,1,0:T(8,128)S(1)}, /*in...) while((s32[]{:T(128)}, f32[3,4,8,256]{3,2,1,0:T(8,128)S(1)}, ...), condition=%wide.region_8.9_spmd, body=%wide.region_3.8_spmd.sunk | while | flops 172047 | bytes 665472 | solution.py:74
  87.3 26.6 %while.162 = (s32[]{:T(128)}, f32[3,4,8,256]{3,2,1,0:T(8,128)S(1)}, f32[3,4,256]{2,1,0:T(4,128)S(1)}, s32[]{:T(128)}, f32[3,4,8,256]{3,2,1,0:T(8,128)S(1)}, /*in...) while((s32[]{:T(128)}, f32[3,4,8,256]{3,2,1,0:T(8,128)S(1)}, ...), condition=%wide.region_14.15_spmd, body=%wide.region_9.14_spmd.sunk | while | flops 172047 | bytes 665472 | solution.py:74
  121.4 16.3 %scatter_custom_fusion.8 = s32[8192]{0:T(1024)} fusion(s32[4096]{0:T(1024)S(1)} %broadcast_select_fusion, s32[4096]{0:T(1024)} %bitcast.782, s32[]{:T(128)} %constant.1186.clone.1), kind=kCustom, calls=%fused_computation.380 | custom fusion | bytes 33280
  146.7 16.3 %gather_fusion = f32[4096,3]{1,0:T(8,128)} fusion(f32[3,8192]{0,1:T(8,128)} %bitcast.749, s32[4096]{0:T(1024)S(1)} %broadcast_clamp_fusion), kind=kCustom, calls=%fused_computation | custom fusion | bytes 114688 | tf_op jit(solution)/shard_map/gather | solution.py:168
  176.1 13.1 %scatter_custom_fusion = f32[3,8192]{0,1:T(8,128)} fusion(s32[4096]{0:T(1024)S(1)} %bitcast.771, f32[4096,3]{1,0:T(8,128)} %copy.146, f32[]{:T(128)} %constant.1184.clone.1), kind=kCustom, calls=%fused_computation.195 | custom fusion | bytes 98816 | tf_op jit(solution)/shard_map/scatter | solution.py:169
  213.9 55.9 %scatter_fusion = f32[3,8192]{0,1:T(8,128)} fusion(f32[3,8192]{0,1:T(8,128)} %bitcast.737, s32[8192]{0:T(1024)S(1)} %bitcast.757, f32[8192,3]{1,0:T(8,128)} %copy.148), kind=kCustom, calls=%fused_computation.5 | custom fusion | flops 24576 | bytes 327680 | tf_op jit(solution)/shard_map/scatter-add | solution.py:174
  281.7 19.5 %all-reduce.9 = (f32[]{:T(128)}, f32[1]{0:T(128)}) all-reduce(f32[]{:T(128)} %get-tuple-element.1666, f32[1]{0:T(128)} %get-tuple-element.1667), channel_id=1, replica_groups=mesh['areal'=8,'layer'=4] {'areal'}, use_global_device_ids=true, to_apply=%region_34.35 | all-reduce | flops 2 | bytes 16 | tf_op jit(solution)/shard_map/psum | solution.py:13
  303.9 23.9 %while.163 = (s32[]{:T(128)}, f32[3,4,8,256]{3,2,1,0:T(8,128)S(1)}, f32[3,4,256]{2,1,0:T(4,128)S(1)}, s32[]{:T(128)}, f32[3,4,8,256]{3,2,1,0:T(8,128)S(1)}, /*in...) while((s32[]{:T(128)}, f32[3,4,8,256]{3,2,1,0:T(8,128)S(1)}, ...), condition=%wide.region_42.43_spmd, body=%wide.region_37.42_spmd.sunk | while | flops 172047 | bytes 665472 | solution.py:74
  327.8 26.6 %while.164 = (s32[]{:T(128)}, f32[3,4,8,256]{3,2,1,0:T(8,128)S(1)}, f32[3,4,256]{2,1,0:T(4,128)S(1)}, s32[]{:T(128)}, f32[3,4,8,256]{3,2,1,0:T(8,128)S(1)}, /*in...) while((s32[]{:T(128)}, f32[3,4,8,256]{3,2,1,0:T(8,128)S(1)}, ...), condition=%wide.region_48.49_spmd, body=%wide.region_43.48_spmd.sunk | while | flops 172047 | bytes 665472 | solution.py:74
  360.6 16.3 %gather_fusion.1 = f32[4096,3]{1,0:T(8,128)} fusion(f32[3,8192]{0,1:T(8,128)} %bitcast.752, s32[4096]{0:T(1024)S(1)} %broadcast_clamp_fusion), kind=kCustom, calls=%fused_computation.1 | custom fusion | bytes 114688 | tf_op jit(solution)/shard_map/gather | solution.py:168
  417.7 55.8 %scatter_fusion.1 = f32[3,8192]{0,1:T(8,128)} fusion(f32[3,8192]{0,1:T(8,128)} %bitcast.741, s32[8192]{0:T(1024)S(1)} %bitcast.758, f32[8192,3]{1,0:T(8,128)} %copy.157), kind=kCustom, calls=%fused_computation.7 | custom fusion | flops 24576 | bytes 327680 | tf_op jit(solution)/shard_map/scatter-add | solution.py:174
  485.2 19.9 %all-reduce.8 = (f32[]{:T(128)}, f32[2]{0:T(128)S(1)}) all-reduce(f32[]{:T(128)} %get-tuple-element.1664, f32[2]{0:T(128)S(1)} %get-tuple-element.1665), channel_id=1, replica_groups=mesh['areal'=8,'layer'=4] {'areal'}, use_global_device_ids=true, to_apply=%region_65.66 | all-reduce | flops 3 | bytes 24 | tf_op jit(solution)/shard_map/psum | solution.py:13
  509.0 23.9 %while.165 = (s32[]{:T(128)}, f32[3,4,8,256]{3,2,1,0:T(8,128)S(1)}, f32[3,4,256]{2,1,0:T(4,128)S(1)}, s32[]{:T(128)}, f32[3,4,8,256]{3,2,1,0:T(8,128)S(1)}, /*in...) while((s32[]{:T(128)}, f32[3,4,8,256]{3,2,1,0:T(8,128)S(1)}, ...), condition=%wide.region_74.75_spmd, body=%wide.region_69.74_spmd.sunk | while | flops 172047 | bytes 665472 | solution.py:74
  533.0 26.6 %while.166 = (s32[]{:T(128)}, f32[3,4,8,256]{3,2,1,0:T(8,128)S(1)}, f32[3,4,256]{2,1,0:T(4,128)S(1)}, s32[]{:T(128)}, f32[3,4,8,256]{3,2,1,0:T(8,128)S(1)}, /*in...) while((s32[]{:T(128)}, f32[3,4,8,256]{3,2,1,0:T(8,128)S(1)}, ...), condition=%wide.region_80.81_spmd, body=%wide.region_75.0_spmd.sunk | while | flops 172047 | bytes 665472 | solution.py:74
  562.3 16.3 %gather_fusion.2 = f32[4096,3]{1,0:T(8,128)} fusion(f32[3,8192]{0,1:T(8,128)} %bitcast.751, s32[4096]{0:T(1024)S(1)} %broadcast_clamp_fusion), kind=kCustom, calls=%fused_computation.2 | custom fusion | bytes 114688 | tf_op jit(solution)/shard_map/gather | solution.py:168
  620.9 55.8 %scatter_fusion.2 = f32[3,8192]{0,1:T(8,128)} fusion(f32[3,8192]{0,1:T(8,128)} %bitcast.743, s32[8192]{0:T(1024)S(1)} %bitcast.759, f32[8192,3]{1,0:T(8,128)} %copy.166), kind=kCustom, calls=%fused_computation.9 | custom fusion | flops 24576 | bytes 327680 | tf_op jit(solution)/shard_map/scatter-add | solution.py:174
  690.3 23.1 %all-reduce.7 = (f32[]{:T(128)}, f32[3]{0:T(128)S(1)}) all-reduce(f32[]{:T(128)} %get-tuple-element.1662, f32[3]{0:T(128)S(1)} %get-tuple-element.1663), channel_id=1, replica_groups=mesh['areal'=8,'layer'=4] {'areal'}, use_global_device_ids=true, to_apply=%region_98.99 | all-reduce | flops 4 | bytes 32 | tf_op jit(solution)/shard_map/psum | solution.py:13
  718.0 23.9 %while.167 = (s32[]{:T(128)}, f32[3,4,8,256]{3,2,1,0:T(8,128)S(1)}, f32[3,4,256]{2,1,0:T(4,128)S(1)}, s32[]{:T(128)}, f32[3,4,8,256]{3,2,1,0:T(8,128)S(1)}, /*in...) while((s32[]{:T(128)}, f32[3,4,8,256]{3,2,1,0:T(8,128)S(1)}, ...), condition=%wide.region_107.108_spmd, body=%wide.region_102.107_spmd.sunk | while | flops 172047 | bytes 665472 | solution.py:74
  742.0 26.6 %while.168 = (s32[]{:T(128)}, f32[3,4,8,256]{3,2,1,0:T(8,128)S(1)}, f32[3,4,256]{2,1,0:T(4,128)S(1)}, s32[]{:T(128)}, f32[3,4,8,256]{3,2,1,0:T(8,128)S(1)}, /*in...) while((s32[]{:T(128)}, f32[3,4,8,256]{3,2,1,0:T(8,128)S(1)}, ...), condition=%wide.region_113.114_spmd, body=%wide.region_108.0_spmd.sunk | while | flops 172047 | bytes 665472 | solution.py:74
  771.2 16.3 %gather_fusion.3 = f32[4096,3]{1,0:T(8,128)} fusion(f32[3,8192]{0,1:T(8,128)} %bitcast.750, s32[4096]{0:T(1024)S(1)} %broadcast_clamp_fusion), kind=kCustom, calls=%fused_computation.3 | custom fusion | bytes 114688 | tf_op jit(solution)/shard_map/gather | solution.py:168
  794.4 13.2 %scatter_custom_fusion.6 = f32[3,8192]{0,1:T(8,128)} fusion(s32[4096]{0:T(1024)S(1)} %bitcast.774, f32[4096,3]{1,0:T(8,128)} %copy.173, f32[]{:T(128)} %constant.1184.clone.1), kind=kCustom, calls=%fused_computation.189 | custom fusion | bytes 98816 | tf_op jit(solution)/shard_map/scatter | solution.py:169
  829.8 55.8 %scatter_fusion.3 = f32[3,8192]{0,1:T(8,128)} fusion(f32[3,8192]{0,1:T(8,128)} %bitcast.739, s32[8192]{0:T(1024)S(1)} %bitcast.760, f32[8192,3]{1,0:T(8,128)} %copy.175), kind=kCustom, calls=%fused_computation.11 | custom fusion | flops 24576 | bytes 327680 | tf_op jit(solution)/shard_map/scatter-add | solution.py:174
  899.8 23.1 %all-reduce.6 = (f32[4]{0:T(128)S(1)}, f32[]{:T(128)}) all-reduce(f32[4]{0:T(128)S(1)} %get-tuple-element.1660, f32[]{:T(128)} %get-tuple-element.1661), channel_id=1, replica_groups=mesh['areal'=8,'layer'=4] {'areal'}, use_global_device_ids=true, to_apply=%region_129.130 | all-reduce | flops 5 | bytes 40 | tf_op jit(solution)/shard_map/psum | solution.py:13
  (735 shorter events, 467.8 us)
Async XLA Ops:
  56.6 5.7 collective-permute-start
  92.7 5.6 collective-permute-start.1
  114.0 54.0 %collective-permute-start.8 = (f32[3,4,1,256]{3,2,1,0:T(1,128)S(1)}, f32[3,4,1,256]{3,2,1,0:T(1,128)S(1)}, u32[]{:S(2)}, u32[]{:S(2)}) collective-permute-start(f32[3,4,1,256]{3,2,1,0:T(1,128)S(1)} %get-tuple-element.1741), channel_id=1, source_target_pairs={{0,4},{4,8},{8,12},{12,16},{16,20},{20,24},{24,28},{1,5},{5,9},{9,... | collective-permute-start | bytes 36872 | tf_op jit(solution)/shard_map/ppermute | solution.py:27
  116.7 51.2 %collective-permute-start.9 = (f32[3,4,1,256]{3,2,1,0:T(1,128)S(1)}, f32[3,4,1,256]{3,2,1,0:T(1,128)S(1)}, u32[]{:S(2)}, u32[]{:S(2)}) collective-permute-start(f32[3,4,1,256]{3,2,1,0:T(1,128)S(1)} %get-tuple-element.1742), channel_id=1, source_target_pairs={{4,0},{8,4},{12,8},{16,12},{20,16},{24,20},{28,24},{5,1},{9,5},{13... | collective-permute-start | bytes 36872 | tf_op jit(solution)/shard_map/ppermute | solution.py:30
  137.7 60.2 %all-to-all-start = ((s32[1,8,1024]{2,0,1:T(1,128)}), s32[1,8,1024]{2,0,1:T(1,128)S(1)}, u32[]{:S(2)}, u32[]{:S(2)}) async-start(s32[1,8,1024]{2,0,1:T(1,128)} %bitcast.141), calls=%async_computation | async-start | bytes 65536 | tf_op jit(solution)/shard_map/all_to_all | solution.py:144
  168.0 26.6 %collective-permute-start.10 = (f32[3,1,10,256]{3,2,1,0:T(8,128)S(1)}, f32[3,1,10,256]{3,2,1,0:T(8,128)S(1)}, u32[]{:S(2)}, u32[]{:S(2)}) collective-permute-start(f32[3,1,10,256]{3,2,1,0:T(8,128)S(1)} %get-tuple-element.1726), channel_id=1, source_target_pairs={{0,1},{1,2},{2,3},{4,5},{5,6},{6,7},{8,9},{9,10},{10,11},{12,13},{... | collective-permute-start | bytes 92168 | tf_op jit(solution)/shard_map/ppermute | solution.py:27
  171.5 23.1 %collective-permute-start.11 = (f32[3,1,10,256]{3,2,1,0:T(8,128)S(1)}, f32[3,1,10,256]{3,2,1,0:T(8,128)S(1)}, u32[]{:S(2)}, u32[]{:S(2)}) collective-permute-start(f32[3,1,10,256]{3,2,1,0:T(8,128)S(1)} %get-tuple-element.1725), channel_id=1, source_target_pairs={{1,0},{2,1},{3,2},{5,4},{6,5},{7,6},{9,8},{10,9},{11,10},{13,12},{... | collective-permute-start | bytes 92168 | tf_op jit(solution)/shard_map/ppermute | solution.py:30
  197.8 13.5 %all-to-all-start.1 = ((f32[3,8,1024]{2,0,1:T(4,128)}), f32[3,8,1024]{2,0,1:T(4,128)S(1)}, u32[]{:S(2)}, u32[]{:S(2)}) async-start(f32[3,8,1024]{2,0,1:T(4,128)} %copy.147), calls=%async_computation.1 | async-start | bytes 262144 | tf_op jit(solution)/shard_map/all_to_all | solution.py:170
  306.4 5.7 collective-permute-start.2
  354.5 24.6 %collective-permute-start.12 = (f32[3,4,1,256]{3,2,1,0:T(1,128)S(1)}, f32[3,4,1,256]{3,2,1,0:T(1,128)S(1)}, u32[]{:S(2)}, u32[]{:S(2)}) collective-permute-start(f32[3,4,1,256]{3,2,1,0:T(1,128)S(1)} %get-tuple-element.1739), channel_id=1, source_target_pairs={{0,4},{4,8},{8,12},{12,16},{16,20},{20,24},{24,28},{1,5},{5,9},{9,... | collective-permute-start | bytes 36872 | tf_op jit(solution)/shard_map/ppermute | solution.py:27
  356.7 22.4 %collective-permute-start.13 = (f32[3,4,1,256]{3,2,1,0:T(1,128)S(1)}, f32[3,4,1,256]{3,2,1,0:T(1,128)S(1)}, u32[]{:S(2)}, u32[]{:S(2)}) collective-permute-start(f32[3,4,1,256]{3,2,1,0:T(1,128)S(1)} %get-tuple-element.1740), channel_id=1, source_target_pairs={{4,0},{8,4},{12,8},{16,12},{20,16},{24,20},{28,24},{5,1},{9,5},{13... | collective-permute-start | bytes 36872 | tf_op jit(solution)/shard_map/ppermute | solution.py:30
  379.1 28.4 %collective-permute-start.14 = (f32[3,1,10,256]{3,2,1,0:T(8,128)S(1)}, f32[3,1,10,256]{3,2,1,0:T(8,128)S(1)}, u32[]{:S(2)}, u32[]{:S(2)}) collective-permute-start(f32[3,1,10,256]{3,2,1,0:T(8,128)S(1)} %get-tuple-element.1722), channel_id=1, source_target_pairs={{0,1},{1,2},{2,3},{4,5},{5,6},{6,7},{8,9},{9,10},{10,11},{12,13},{... | collective-permute-start | bytes 92168 | tf_op jit(solution)/shard_map/ppermute | solution.py:27
  383.2 24.4 %collective-permute-start.15 = (f32[3,1,10,256]{3,2,1,0:T(8,128)S(1)}, f32[3,1,10,256]{3,2,1,0:T(8,128)S(1)}, u32[]{:S(2)}, u32[]{:S(2)}) collective-permute-start(f32[3,1,10,256]{3,2,1,0:T(8,128)S(1)} %get-tuple-element.1721), channel_id=1, source_target_pairs={{1,0},{2,1},{3,2},{5,4},{6,5},{7,6},{9,8},{10,9},{11,10},{13,12},{... | collective-permute-start | bytes 92168 | tf_op jit(solution)/shard_map/ppermute | solution.py:30
  403.2 11.9 %all-to-all-start.2 = ((f32[3,8,1024]{2,0,1:T(4,128)}), f32[3,8,1024]{2,0,1:T(4,128)S(1)}, u32[]{:S(2)}, u32[]{:S(2)}) async-start(f32[3,8,1024]{2,0,1:T(4,128)} %copy.156), calls=%async_computation.2 | async-start | bytes 262144 | tf_op jit(solution)/shard_map/all_to_all | solution.py:170
  511.6 5.7 collective-permute-start.4
  580.8 25.8 %collective-permute-start.16 = (f32[3,4,1,256]{3,2,1,0:T(1,128)S(1)}, f32[3,4,1,256]{3,2,1,0:T(1,128)S(1)}, u32[]{:S(2)}, u32[]{:S(2)}) collective-permute-start(f32[3,4,1,256]{3,2,1,0:T(1,128)S(1)} %get-tuple-element.1737), channel_id=1, source_target_pairs={{0,4},{4,8},{8,12},{12,16},{16,20},{20,24},{24,28},{1,5},{5,9},{9,... | collective-permute-start | bytes 36872 | tf_op jit(solution)/shard_map/ppermute | solution.py:27
  582.5 24.0 %collective-permute-start.17 = (f32[3,4,1,256]{3,2,1,0:T(1,128)S(1)}, f32[3,4,1,256]{3,2,1,0:T(1,128)S(1)}, u32[]{:S(2)}, u32[]{:S(2)}) collective-permute-start(f32[3,4,1,256]{3,2,1,0:T(1,128)S(1)} %get-tuple-element.1738), channel_id=1, source_target_pairs={{4,0},{8,4},{12,8},{16,12},{20,16},{24,20},{28,24},{5,1},{9,5},{13... | collective-permute-start | bytes 36872 | tf_op jit(solution)/shard_map/ppermute | solution.py:30
  602.7 15.6 %all-to-all-start.3 = ((f32[3,8,1024]{2,0,1:T(4,128)}), f32[3,8,1024]{2,0,1:T(4,128)S(1)}, u32[]{:S(2)}, u32[]{:S(2)}) async-start(f32[3,8,1024]{2,0,1:T(4,128)} %copy.165), calls=%async_computation.3 | async-start | bytes 262144 | tf_op jit(solution)/shard_map/all_to_all | solution.py:170
  606.6 8.3 collective-permute-start.18
  720.6 5.7 collective-permute-start.6
  789.7 25.7 %collective-permute-start.20 = (f32[3,4,1,256]{3,2,1,0:T(1,128)S(1)}, f32[3,4,1,256]{3,2,1,0:T(1,128)S(1)}, u32[]{:S(2)}, u32[]{:S(2)}) collective-permute-start(f32[3,4,1,256]{3,2,1,0:T(1,128)S(1)} %get-tuple-element.1735), channel_id=1, source_target_pairs={{0,4},{4,8},{8,12},{12,16},{16,20},{20,24},{24,28},{1,5},{5,9},{9,... | collective-permute-start | bytes 36872 | tf_op jit(solution)/shard_map/ppermute | solution.py:27
  791.0 24.4 %collective-permute-start.21 = (f32[3,4,1,256]{3,2,1,0:T(1,128)S(1)}, f32[3,4,1,256]{3,2,1,0:T(1,128)S(1)}, u32[]{:S(2)}, u32[]{:S(2)}) collective-permute-start(f32[3,4,1,256]{3,2,1,0:T(1,128)S(1)} %get-tuple-element.1736), channel_id=1, source_target_pairs={{4,0},{8,4},{12,8},{16,12},{20,16},{24,20},{28,24},{5,1},{9,5},{13... | collective-permute-start | bytes 36872 | tf_op jit(solution)/shard_map/ppermute | solution.py:30
  811.2 16.0 %all-to-all-start.4 = ((f32[3,8,1024]{2,0,1:T(4,128)}), f32[3,8,1024]{2,0,1:T(4,128)S(1)}, u32[]{:S(2)}, u32[]{:S(2)}) async-start(f32[3,8,1024]{2,0,1:T(4,128)} %copy.174), calls=%async_computation.4 | async-start | bytes 262144 | tf_op jit(solution)/shard_map/all_to_all | solution.py:170
  815.5 8.3 collective-permute-start.22
  (52 other events, 1136.3 us)
